TPU v7x, 128 devices: a whole 4x4x4 slice. The times are simulated.
128 devices in a mesh: ctxa: 8 (over x, core), ctxb: 16 (over z, y).
Axes of the slice: x: 4, y: 4, z: 4, core: 2. Of those that a mesh axis runs over, the one named last changes fastest.
Arguments:
- tokens: bfloat16 [65536, 2048], P(('ctxa', 'ctxb')), may hold values from -6 to 6
- cotangent: bfloat16 [65536, 2048], P(('ctxa', 'ctxb')), may hold values from -6 to 6
- w_query: bfloat16 [2048, 1024], replicated, may hold values from -0.125 to 0.125
- w_key: bfloat16 [2048, 1024], replicated, may hold values from -0.125 to 0.125
- w_value: bfloat16 [2048, 1024], replicated, may hold values from -0.125 to 0.125
- w_out: bfloat16 [1024, 2048], replicated, may hold values from -0.125 to 0.125
Outputs:
- grad_tokens: bfloat16 [65536, 2048], P(('ctxa', 'ctxb'))
All inputs are finite; a program needn't handle non-finite values.
Results may differ from a plain program's by a relative error of at most 0.012.
Values may be sent and summed in bfloat16 or wider, within the bound.
A program may use at most 256 MiB of HBM per device.

v0:
```python
import math
import jax
import jax.numpy as jnp
from jax import lax
from jax.sharding import PartitionSpec as P

H = 8
DH = 128


def prefix(x, axis, join, neutral, backward):
    count = lax.axis_size(axis)
    place = lax.axis_index(axis)
    ahead = count - 1 - place if backward else place
    gathered = lax.all_gather(x.astype(jnp.bfloat16), axis)
    state = jnp.zeros_like(x) + jnp.asarray(neutral, x.dtype)

    def one(lap, state):
        source = count - 1 - lap if backward else lap
        return join(state, lax.dynamic_index_in_dim(gathered, source, 0, False).astype(x.dtype))

    return lax.fori_loop(0, ahead, one, state)


def project(left, weight):
    return jnp.dot(left, weight, preferred_element_type=jnp.float32).astype(jnp.bfloat16)


def add_states(earlier, later):
    return earlier + later


def regrouped_states(key_state, grad_state):
    key_group, grad_group = (
        lax.all_to_all(key_state[None], "ctxa", split_axis=1, concat_axis=0, tiled=True),
        lax.all_to_all(grad_state[None], "ctxa", split_axis=1, concat_axis=0, tiled=True),
    )
    key_total, grad_total = lax.psum((key_group, grad_group), "ctxb")
    key_row = prefix(key_group, "ctxb", add_states, jnp.zeros_like(key_group), False)
    grad_row = prefix(grad_group, "ctxb", add_states, jnp.zeros_like(grad_group), True)
    key_prior = jnp.cumsum(key_total, axis=0) - key_total + key_row
    grad_later = (
        jnp.sum(grad_total, axis=0, keepdims=True) - jnp.cumsum(grad_total, axis=0) + grad_row
    )
    key_prior = key_prior.astype(jnp.bfloat16)
    grad_later = grad_later.astype(jnp.bfloat16)
    returned = (
        lax.all_to_all(key_prior, "ctxa", split_axis=0, concat_axis=1, tiled=True),
        lax.all_to_all(grad_later, "ctxa", split_axis=0, concat_axis=1, tiled=True),
    )
    return (returned[0][0], returned[1][0])


def shards(tokens, cotangent, w_query, w_key, w_value, w_out):
    rows = tokens.shape[0]
    factor = 1.0 / math.sqrt(DH * rows * lax.axis_size("ctxa") * lax.axis_size("ctxb"))
    query = project(tokens, w_query).reshape(rows, H, DH)
    keys = project(tokens, w_key).reshape(rows, H, DH)
    values = project(tokens, w_value).reshape(rows, H, DH)
    grad_out = lax.dot_general(
        cotangent, w_out, (((1,), (1,)), ((), ())), preferred_element_type=jnp.float32
    )
    grad_out = grad_out.astype(jnp.bfloat16).reshape(rows, H, DH)
    key_state = jnp.einsum("rhi,rhj->hij", keys, values, preferred_element_type=jnp.float32)
    grad_state = jnp.einsum("rhi,rhj->hij", query, grad_out, preferred_element_type=jnp.float32)
    prior, later = regrouped_states(key_state, grad_state)
    index = jnp.arange(rows)
    causal = (index[:, None] >= index[None, :])[None]
    attend = jnp.where(
        causal, jnp.einsum("thi,shi->hts", query, keys, preferred_element_type=jnp.float32), 0.0
    ).astype(jnp.bfloat16)
    probe = jnp.where(
        causal,
        jnp.einsum("thj,shj->hts", grad_out, values, preferred_element_type=jnp.float32),
        0.0,
    ).astype(jnp.bfloat16)
    grad_query = jnp.einsum("hts,shi->thi", probe, keys, preferred_element_type=jnp.float32)
    grad_query = grad_query + jnp.einsum(
        "thj,hij->thi", grad_out, prior, preferred_element_type=jnp.float32
    )
    grad_key = jnp.einsum("hts,thi->shi", probe, query, preferred_element_type=jnp.float32)
    grad_key = grad_key + jnp.einsum(
        "shj,hij->shi", values, later, preferred_element_type=jnp.float32
    )
    grad_value = jnp.einsum("hts,thj->shj", attend, grad_out, preferred_element_type=jnp.float32)
    grad_value = grad_value + jnp.einsum(
        "shi,hij->shj", keys, later, preferred_element_type=jnp.float32
    )

    def finish(partial_grad):
        return (factor * partial_grad).astype(jnp.bfloat16).reshape(rows, H * DH)

    total = jnp.dot(finish(grad_query), w_query.T, preferred_element_type=jnp.float32)
    total = total + jnp.dot(finish(grad_key), w_key.T, preferred_element_type=jnp.float32)
    total = total + jnp.dot(finish(grad_value), w_value.T, preferred_element_type=jnp.float32)
    return total.astype(jnp.bfloat16)


def solution(mesh):
    placed = (P(("ctxa", "ctxb"), None), P(("ctxa", "ctxb"), None), P(), P(), P(), P())
    return jax.shard_map(
        shards, mesh=mesh, in_specs=placed, out_specs=P(("ctxa", "ctxb"), None), check_vma=False
    )
```

profile of v0, /device:TPU:1, one launch (start us, length us, event | category | flops | bytes accessed | tf_op | source)
XLA Modules:
  0.0 311.3 jit_solution(6295105417670766009)
XLA Ops:
  6.5 1.6 copy-done
  8.1 4.8 %fusion.5 = bf16[64,8,8,128]{3,2,1,0:T(8,128)(2,1)S(1)} fusion(bf16[512,2048]{1,0:T(8,128)(2,1)S(1)} %copy-done, bf16[2048,1024]{1,0:T(8,128)(2,1)} %param.13), kind=kOutput, calls=%fused_computation.16 | convolution fusion | flops 2148007936 | bytes 7340032 | tf_op jit(solution)/shard_map/dot_general | solution.py:26
  12.9 2.4 fusion.6
  16.3 1.4 convolution_bitcast_fusion.1
  17.7 5.8 %all-to-all-start = ((f32[1,8,128,128]{3,2,0,1:T(8,128)}), f32[1,8,128,128]{3,2,0,1:T(8,128)}, u32[]{:S(2)}, u32[]{:S(2)}) async-start(f32[1,8,128,128]{3,2,0,1:T(8,128)} %convolution_bitcast_fusion.1), calls=%async_computation | async-start | bytes 1048576 | tf_op jit(solution)/shard_map/all_to_all | solution.py:35
  23.5 5.6 %fusion.7 = bf16[64,8,8,128]{3,2,1,0:T(8,128)(2,1)} fusion(bf16[512,2048]{1,0:T(8,128)(2,1)S(1)} %copy-done, bf16[2048,1024]{1,0:T(8,128)(2,1)} %param.12), kind=kOutput, calls=%fused_computation.18 | convolution fusion | flops 2148007936 | bytes 7340032 | tf_op jit(solution)/shard_map/dot_general | solution.py:26
  29.1 3.3 %convolution_convert_fusion.2 = bf16[512,1024]{1,0:T(8,128)(2,1)} fusion(bf16[512,2048]{1,0:T(8,128)(2,1)S(1)} %copy-done.14, bf16[1024,2048]{1,0:T(8,128)(2,1)S(1)} %copy-done.9), kind=kOutput, calls=%fused_computation.14 | convolution fusion | flops 2148007936 | bytes 7340032 | tf_op jit(solution)/shard_map/dot_general | solution.py:60
  32.4 1.5 copy.49
  34.0 2.9 convolution_bitcast_fusion
  36.9 4.8 %all-to-all-start.2 = ((f32[1,8,128,128]{3,2,0,1:T(8,128)}), f32[1,8,128,128]{3,2,0,1:T(8,128)}, u32[]{:S(2)}, u32[]{:S(2)}) async-start(f32[1,8,128,128]{3,2,0,1:T(8,128)} %convolution_bitcast_fusion), calls=%async_computation.2 | async-start | bytes 1048576 | tf_op jit(solution)/shard_map/all_to_all | solution.py:36
  41.7 1.8 convert_bitcast_fusion.1
  43.5 7.7 %all-to-all-done.2 = f32[1,8,128,128]{3,2,0,1:T(8,128)} async-done(((f32[1,8,128,128]{3,2,0,1:T(8,128)}), f32[1,8,128,128]{3,2,0,1:T(8,128)}, u32[]{:S(2)}, u32[]{:S(2)}) %all-to-all-start.2) | async-done | bytes 524320 | tf_op jit(solution)/shard_map/all_to_all | solution.py:36
  51.1 1.8 convert_bitcast_fusion
  55.2 2.7 select_convert_fusion.1
  57.9 2.1 fusion.15
  60.1 2.9 fusion.25
  62.9 4.9 %fusion = f32[8,128,512]{2,1,0:T(8,128)} fusion(bf16[512,8,128]{0,2,1:T(8,128)(2,1)S(1)} %bitcast.111, pred[512,512]{1,0:T(8,128)(4,1)S(1)} %iota_compare_fusion, bf16[64,8,8,128]{3,2,1,0:T(8,128)(2,1)} %fusion.7, bf16[64,8,8,128]{3,2,1,0:T(8,128)(2,1)} %copy-done.2), kind=kOutput, calls=%fused_computation.4 | convolution fusion | flops 1077936128 | bytes 5505024 | tf_op jit(solution)/shard_map/hts,thj->shj/dot_general | solution.py:85
  67.8 76.2 %all-reduce.3.cloned.1.call-done = (f32[8,1,128,128]{3,2,0,1:T(8,128)}, f32[8,1,128,128]{3,2,0,1:T(8,128)}) async-done(((f32[8,1,128,128]{3,2,0,1:T(8,128)}, f32[8,1,128,128]{3,2,0,1:T(8,128)}), (f32[8,1,128,128]{3,2,0,1:T(8,128)}, f32[8,1,128,128]{3,2,0,1:T(8,128)})) %all-reduce.3.cloned.1.call-update) | async-done | bytes 1048592 | tf_op jit(solution)/shard_map/psum | solution.py:38
  144.0 1.1 reduce_sum.9
  145.1 53.2 %all-gather.5.cloned.1.call-done = bf16[16,8,128,128]{3,2,1,0:T(8,128)(2,1)} async-done(((bf16[1,8,128,128]{3,2,1,0:T(8,128)(2,1)}), bf16[16,8,128,128]{3,2,1,0:T(8,128)(2,1)}) %all-gather.5.cloned.1.call-update) | async-done | bytes 4194320 | tf_op jit(solution)/shard_map/all_gather | solution.py:15
  198.4 53.2 %all-gather.7.cloned.1.call-done = bf16[16,8,128,128]{3,2,1,0:T(8,128)(2,1)} async-done(((bf16[1,8,128,128]{3,2,1,0:T(8,128)(2,1)}), bf16[16,8,128,128]{3,2,1,0:T(8,128)(2,1)}) %all-gather.7.cloned.1.call-update) | async-done | bytes 4194320 | tf_op jit(solution)/shard_map/all_gather | solution.py:15
  251.6 16.4 %while.23 = (s32[]{:T(128)}, f32[8,1,128,128]{3,2,1,0:T(8,128)S(1)}, s32[]{:T(128)}, bf16[16,8,1,128,128]{4,3,1,2,0:T(8,128)(2,1)}, s32[]{:T(128)}, /*index=5*/s32[]{:T(128)}, s32[]{:T(128)}, s32[]{:T(128)}) while((s32[]{:T(128)}, f32[8,1,128,128]{3,2,1,0:T(8,128)S(1)}, s32[]{:T(128)}, bf16[16,8,1,128,128]{4,3,1,2,0:T(8,128)(2,1)}, s32[]{:T(128)}, ...), condition=%wide.region_8.9_spmd, body=%wide.region_7.8_spmd.sunk | while | flops 262150 | bytes 1310863 | solution.py:22
  251.7 1.1 convert_add_fusion.5
  252.8 1.1 convert_add_fusion.5
  253.9 1.1 convert_add_fusion.5
  254.9 1.1 convert_add_fusion.5
  256.0 1.1 convert_add_fusion.5
  257.1 1.1 convert_add_fusion.5
  258.2 1.1 convert_add_fusion.5
  259.3 1.1 convert_add_fusion.5
  260.4 1.1 convert_add_fusion.5
  261.5 1.1 convert_add_fusion.5
  262.6 1.1 convert_add_fusion.5
  263.7 1.1 convert_add_fusion.5
  264.8 1.1 convert_add_fusion.5
  265.9 1.1 convert_add_fusion.5
  267.0 1.1 convert_add_fusion.5
  268.0 2.0 fusion.11
  270.0 5.1 %all-to-all-start.1 = ((bf16[8,1,128,128]{3,2,1,0:T(8,128)(2,1)}), bf16[8,1,128,128]{3,2,1,0:T(8,128)(2,1)S(1)}, u32[]{:S(2)}, u32[]{:S(2)}) async-start(bf16[8,1,128,128]{3,2,1,0:T(8,128)(2,1)} %fusion.11), calls=%async_computation.1 | async-start | bytes 524288 | tf_op jit(solution)/shard_map/all_to_all | solution.py:48
  275.1 1.8 fusion.13
  276.9 4.7 %all-to-all-done.1 = bf16[8,1,128,128]{3,2,1,0:T(8,128)(2,1)S(1)} async-done(((bf16[8,1,128,128]{3,2,1,0:T(8,128)(2,1)}), bf16[8,1,128,128]{3,2,1,0:T(8,128)(2,1)S(1)}, u32[]{:S(2)}, u32[]{:S(2)}) %all-to-all-start.1) | async-done | bytes 262176 | tf_op jit(solution)/shard_map/all_to_all | solution.py:48
  281.6 4.4 %all-to-all-start.3 = ((bf16[8,1,128,128]{3,2,1,0:T(8,128)(2,1)}), bf16[8,1,128,128]{3,2,1,0:T(8,128)(2,1)S(1)}, u32[]{:S(2)}, u32[]{:S(2)}) async-start(bf16[8,1,128,128]{3,2,1,0:T(8,128)(2,1)} %fusion.13), calls=%async_computation.3 | async-start | bytes 524288 | tf_op jit(solution)/shard_map/all_to_all | solution.py:49
  285.9 2.5 multiply_convert_fusion.2
  289.1 4.3 %fusion.44 = f32[512,2048]{1,0:T(8,128)} fusion(bf16[512,1024]{0,1:T(8,128)(2,1)S(1)} %bitcast.114, bf16[2048,1024]{1,0:T(8,128)(2,1)S(1)} %copy-done.10), kind=kOutput, calls=%fused_computation.58 | convolution fusion | flops 2147483648 | bytes 9437184 | tf_op jit(solution)/shard_map/dot_general | solution.py:93
  293.4 2.2 multiply_convert_fusion.1
  296.2 2.4 fusion.45
  299.4 1.6 copy-done.13
  301.0 3.7 %add_convert_fusion = bf16[512,2048]{1,0:T(8,128)(2,1)} fusion(f32[512,2048]{1,0:T(8,128)S(1)} %copy-done.15, f32[512,2048]{1,0:T(8,128)S(1)} %fusion.45, bf16[512,1024]{0,1:T(8,128)(2,1)S(1)} %bitcast.113, bf16[2048,1024]{1,0:T(8,128)(2,1)S(1)} %copy-done.13), kind=kOutput, calls=%fused_computation.5 | convolution fusion | flops 2150629376 | bytes 15728640 | tf_op jit(solution)/shard_map/dot_general | solution.py:95
  (43 shorter events, 5.3 us)
Async XLA Ops:
  6.5 1.6 copy-start
  6.5 6.4 %copy-start.12 = (bf16[2048,1024]{1,0:T(8,128)(2,1)S(1)}, bf16[2048,1024]{1,0:T(8,128)(2,1)}, u32[]{:S(2)}) copy-start(bf16[2048,1024]{1,0:T(8,128)(2,1)} %param.14) | copy-start | bytes 12582916
  12.9 2.4 copy-start.2
  15.3 1.0 copy-start.7
  17.7 19.2 %all-to-all-start = ((f32[1,8,128,128]{3,2,0,1:T(8,128)}), f32[1,8,128,128]{3,2,0,1:T(8,128)}, u32[]{:S(2)}, u32[]{:S(2)}) async-start(f32[1,8,128,128]{3,2,0,1:T(8,128)} %convolution_bitcast_fusion.1), calls=%async_computation | async-start | bytes 1048576 | tf_op jit(solution)/shard_map/all_to_all | solution.py:35
  23.5 5.6 %copy-start.9 = (bf16[1024,2048]{1,0:T(8,128)(2,1)S(1)}, bf16[1024,2048]{1,0:T(8,128)(2,1)}, u32[]{:S(2)}) copy-start(bf16[1024,2048]{1,0:T(8,128)(2,1)} %param.15) | copy-start | bytes 12582916
  23.5 5.6 %copy-start.14 = (bf16[512,2048]{1,0:T(8,128)(2,1)S(1)}, bf16[512,2048]{1,0:T(8,128)(2,1)}, u32[]{:S(2)}) copy-start(bf16[512,2048]{1,0:T(8,128)(2,1)} %param.11) | copy-start | bytes 6291460
  33.9 29.0 %copy-start.1 = (bf16[512,1024]{0,1:T(8,128)(2,1)}, bf16[512,1024]{0,1:T(8,128)(2,1)S(1)}, u32[]{:S(2)}) copy-start(bf16[512,1024]{0,1:T(8,128)(2,1)S(1)} %copy.49) | copy-start | bytes 3145732
  36.9 14.3 %all-to-all-start.2 = ((f32[1,8,128,128]{3,2,0,1:T(8,128)}), f32[1,8,128,128]{3,2,0,1:T(8,128)}, u32[]{:S(2)}, u32[]{:S(2)}) async-start(f32[1,8,128,128]{3,2,0,1:T(8,128)} %convolution_bitcast_fusion), calls=%async_computation.2 | async-start | bytes 1048576 | tf_op jit(solution)/shard_map/all_to_all | solution.py:36
  52.9 91.1 %all-reduce.3.cloned.1.call-start = ((), (), s32[]{:S(2)}) async-start(), calls=%async_computation.6 | async-start | bytes 2097152 | tf_op jit(solution)/shard_map/psum | solution.py:38
  53.6 144.7 %all-gather.5.cloned.1.call-start = ((), (), s32[]{:S(2)}) async-start(), calls=%async_computation.4 | async-start | bytes 4456448 | tf_op jit(solution)/shard_map/all_gather | solution.py:15
  54.4 197.2 %all-gather.7.cloned.1.call-start = ((), (), s32[]{:S(2)}) async-start(), calls=%async_computation.5 | async-start | bytes 4456448 | tf_op jit(solution)/shard_map/all_gather | solution.py:15
  55.1 2.8 copy-start.5
  57.9 2.2 copy-start.3
  270.0 11.6 %all-to-all-start.1 = ((bf16[8,1,128,128]{3,2,1,0:T(8,128)(2,1)}), bf16[8,1,128,128]{3,2,1,0:T(8,128)(2,1)S(1)}, u32[]{:S(2)}, u32[]{:S(2)}) async-start(bf16[8,1,128,128]{3,2,1,0:T(8,128)(2,1)} %fusion.11), calls=%async_computation.1 | async-start | bytes 524288 | tf_op jit(solution)/shard_map/all_to_all | solution.py:48
  281.6 11.8 %all-to-all-start.3 = ((bf16[8,1,128,128]{3,2,1,0:T(8,128)(2,1)}), bf16[8,1,128,128]{3,2,1,0:T(8,128)(2,1)S(1)}, u32[]{:S(2)}, u32[]{:S(2)}) async-start(bf16[8,1,128,128]{3,2,1,0:T(8,128)(2,1)} %fusion.13), calls=%async_computation.3 | async-start | bytes 524288 | tf_op jit(solution)/shard_map/all_to_all | solution.py:49
  285.9 3.1 %copy-start.10 = (bf16[2048,1024]{1,0:T(8,128)(2,1)S(1)}, bf16[2048,1024]{1,0:T(8,128)(2,1)}, u32[]{:S(2)}) copy-start(bf16[2048,1024]{1,0:T(8,128)(2,1)} %param.12) | copy-start | bytes 12582916
  289.1 4.3 %copy-start.8 = (bf16[64,8,8,128]{3,2,1,0:T(8,128)(2,1)S(1)}, bf16[64,8,8,128]{3,2,1,0:T(8,128)(2,1)}, u32[]{:S(2)}) copy-start(bf16[64,8,8,128]{3,2,1,0:T(8,128)(2,1)} %copy-done.7) | copy-start | bytes 3145732
  293.4 2.8 copy-start.11
  296.2 2.4 copy-start.4
  296.2 2.4 copy-start.6
  296.2 3.2 %copy-start.15 = (f32[512,2048]{1,0:T(8,128)S(1)}, f32[512,2048]{1,0:T(8,128)}, u32[]{:S(2)}) copy-start(f32[512,2048]{1,0:T(8,128)} %fusion.44) | copy-start | bytes 12582916
  298.6 2.4 copy-start.13
Sparse Core Ops, SparseCore 0:
  57.0 86.9 all-reduce.2
  146.2 52.1 all-gather.4
  200.5 51.0 all-gather.6
where the time goes:
time: 313 us; the launch traced here: 311 us
  waiting for transfers between devices  197 us (63%)
  matrix products  48.6 us (16%)
  other arithmetic  24.5 us (8%)
  starting transfers between devices  20.3 us (6%)
  between operations  13.3 us (4%)
  local copies, waits for them, and re-layouts  7.28 us (2%)
    all_gather x2, waiting for transfers between devices, prefix(): gathered = lax.all_gather(x.astype(jnp.bfloat16), axis)  106 us
    psum x1, waiting for transfers between devices, regrouped_states(): key_total, grad_total = lax.psum((key_group, grad_group), 'ctxb')  76.2 us
    add x15, other arithmetic, add_states(): return earlier + later  16 us
    dot_general x3, matrix products, project(): jnp.dot(left, weight, preferred_element_type=jnp.float32)  12.8 us
    all_to_all x1, waiting for transfers between devices, regrouped_states(): lax.all_to_all(grad_state[None], 'ctxa', split_axis=1, concat_axis=0, til...  7.67 us
  transfers between devices with their start and end apart: 7, of which 5 were waited for; matrix products, arithmetic and copies ran while one was open for 12% of the time, Pallas kernels for 0%

commit v1 on v0

--- a/solution.py
+++ b/solution.py
@@ -33,7 +33,12 @@
 def regrouped_states(key_state, grad_state):
     key_group, grad_group = (
         lax.all_to_all(key_state[None], "ctxa", split_axis=1, concat_axis=0, tiled=True),
-        lax.all_to_all(grad_state[None], "ctxa", split_axis=1, concat_axis=0, tiled=True),
+        jnp.concatenate(
+            lax.all_to_all(
+                jnp.stack(jnp.split(grad_state[None], lax.axis_size("ctxa"), axis=1)), "ctxa", 0, 0
+            ),
+            axis=0,
+        ),
     )
     key_total, grad_total = lax.psum((key_group, grad_group), "ctxb")
     key_row = prefix(key_group, "ctxb", add_states, jnp.zeros_like(key_group), False)

time: 313 us -> 317 us (1.013)
  local copies, waits for them, and re-layouts: 7.28 us -> 12.4 us
    unnamed x32 -> x39, local copies, waits for them, and re-layouts: 5.72 us -> 10.2 us
  transfers between devices with their start and end apart: 7 -> 7, of which waited for: 5 -> 5; matrix products, arithmetic and copies ran while one was open for 12% -> 13% of each run, Pallas kernels for 0% -> 0%
where the time goes in v1:
time: 317 us; the launch traced here: 316 us
  waiting for transfers between devices  197 us (62%)
  matrix products  47.8 us (15%)
  other arithmetic  24.5 us (8%)
  starting transfers between devices  20.3 us (6%)
  between operations  13.3 us (4%)
  local copies, waits for them, and re-layouts  12.4 us (4%)
    all_gather x2, waiting for transfers between devices, prefix(): gathered = lax.all_gather(x.astype(jnp.bfloat16), axis)  106 us
    psum x1, waiting for transfers between devices, regrouped_states(): key_total, grad_total = lax.psum((key_group, grad_group), 'ctxb')  76.2 us
    add x15, other arithmetic, add_states(): return earlier + later  16 us
    dot_general x3, matrix products, project(): jnp.dot(left, weight, preferred_element_type=jnp.float32)  12.8 us
    unnamed x39, local copies, waits for them, and re-layouts  10.2 us
    all_to_all x1, waiting for transfers between devices, regrouped_states(): lax.all_to_all(jnp.stack(jnp.split(grad_state[None], lax.axis_size('ctxa'...  7.67 us
  transfers between devices with their start and end apart: 7, of which 5 were waited for; matrix products, arithmetic and copies ran while one was open for 13% of the time, Pallas kernels for 0%

profile of v1, /device:TPU:1, one launch (start us, length us, event | category | flops | bytes accessed | tf_op | source)
XLA Modules:
  0.0 315.6 jit_solution(7136257142909681555)
XLA Ops:
  6.5 1.6 copy-done
  8.1 4.8 %fusion.5 = bf16[64,8,8,128]{3,2,1,0:T(8,128)(2,1)S(1)} fusion(bf16[512,2048]{1,0:T(8,128)(2,1)S(1)} %copy-done, bf16[2048,1024]{1,0:T(8,128)(2,1)} %param.13), kind=kOutput, calls=%fused_computation.16 | convolution fusion | flops 2148007936 | bytes 7340032 | tf_op jit(solution)/shard_map/dot_general | solution.py:26
  12.9 2.4 fusion.6
  16.3 1.4 convolution_bitcast_fusion.1
  17.7 5.8 %all-to-all-start = ((f32[1,8,128,128]{3,2,0,1:T(8,128)}), f32[1,8,128,128]{3,2,0,1:T(8,128)}, u32[]{:S(2)}, u32[]{:S(2)}) async-start(f32[1,8,128,128]{3,2,0,1:T(8,128)} %convolution_bitcast_fusion.1), calls=%async_computation | async-start | bytes 1048576 | tf_op jit(solution)/shard_map/all_to_all | solution.py:35
  23.5 5.6 %fusion.7 = bf16[64,8,8,128]{3,2,1,0:T(8,128)(2,1)} fusion(bf16[512,2048]{1,0:T(8,128)(2,1)S(1)} %copy-done, bf16[2048,1024]{1,0:T(8,128)(2,1)} %param.12), kind=kOutput, calls=%fused_computation.18 | convolution fusion | flops 2148007936 | bytes 7340032 | tf_op jit(solution)/shard_map/dot_general | solution.py:26
  29.1 3.3 %convolution_convert_fusion.2 = bf16[512,1024]{1,0:T(8,128)(2,1)} fusion(bf16[512,2048]{1,0:T(8,128)(2,1)S(1)} %copy-done.14, bf16[1024,2048]{1,0:T(8,128)(2,1)S(1)} %copy-done.9), kind=kOutput, calls=%fused_computation.14 | convolution fusion | flops 2148007936 | bytes 7340032 | tf_op jit(solution)/shard_map/dot_general | solution.py:65
  32.4 1.5 copy.47
  34.0 2.1 convolution_bitcast_fusion
  41.1 4.8 %all-to-all-start.2 = ((f32[8,1,1,128,128]{4,3,2,1,0:T(8,128)}), f32[8,1,1,128,128]{4,3,2,1,0:T(8,128)}, u32[]{:S(2)}, u32[]{:S(2)}) async-start(f32[8,1,1,128,128]{4,3,2,1,0:T(8,128)} %fusion.43), calls=%async_computation.2 | async-start | bytes 1048576 | tf_op jit(solution)/shard_map/all_to_all | solution.py:37
  46.0 1.8 convert_bitcast_fusion
  47.7 7.7 %all-to-all-done.2 = f32[8,1,1,128,128]{4,3,2,1,0:T(8,128)} async-done(((f32[8,1,1,128,128]{4,3,2,1,0:T(8,128)}), f32[8,1,1,128,128]{4,3,2,1,0:T(8,128)}, u32[]{:S(2)}, u32[]{:S(2)}) %all-to-all-start.2) | async-done | bytes 524320 | tf_op jit(solution)/shard_map/all_to_all | solution.py:37
  55.4 1.8 convert_element_type.116
  59.5 2.7 select_convert_fusion.1
  62.2 2.1 fusion.15
  64.4 2.9 fusion.25
  67.2 4.9 %fusion = f32[8,128,512]{2,1,0:T(8,128)} fusion(bf16[512,8,128]{0,2,1:T(8,128)(2,1)S(1)} %bitcast.139, pred[512,512]{1,0:T(8,128)(4,1)S(1)} %iota_compare_fusion, bf16[64,8,8,128]{3,2,1,0:T(8,128)(2,1)} %fusion.7, bf16[64,8,8,128]{3,2,1,0:T(8,128)(2,1)} %copy-done.2), kind=kOutput, calls=%fused_computation.4 | convolution fusion | flops 1077936128 | bytes 5505024 | tf_op jit(solution)/shard_map/hts,thj->shj/dot_general | solution.py:90
  72.1 76.2 %all-reduce.3.cloned.1.call-done = (f32[8,1,128,128]{3,2,0,1:T(8,128)}, f32[8,1,128,128]{3,2,0,1:T(8,128)}) async-done(((f32[8,1,128,128]{3,2,0,1:T(8,128)}, f32[8,1,128,128]{3,2,0,1:T(8,128)}), (f32[8,1,128,128]{3,2,0,1:T(8,128)}, f32[8,1,128,128]{3,2,0,1:T(8,128)})) %all-reduce.3.cloned.1.call-update) | async-done | bytes 1048592 | tf_op jit(solution)/shard_map/psum | solution.py:43
  148.3 1.1 reduce_sum.9
  149.4 53.2 %all-gather.5.cloned.1.call-done = bf16[16,8,128,128]{3,2,1,0:T(8,128)(2,1)} async-done(((bf16[1,8,128,128]{3,2,1,0:T(8,128)(2,1)}), bf16[16,8,128,128]{3,2,1,0:T(8,128)(2,1)}) %all-gather.5.cloned.1.call-update) | async-done | bytes 4194320 | tf_op jit(solution)/shard_map/all_gather | solution.py:15
  202.7 53.2 %all-gather.7.cloned.1.call-done = bf16[128,1,1,128,128]{4,3,2,1,0:T(8,128)(2,1)} async-done(((bf16[8,1,1,128,128]{4,3,2,1,0:T(8,128)(2,1)}), bf16[128,1,1,128,128]{4,3,2,1,0:T(8,128)(2,1)}) %all-gather.7.cloned.1.call-update) | async-done | bytes 4194320 | tf_op jit(solution)/shard_map/all_gather | solution.py:15
  256.0 16.4 %while.23 = (s32[]{:T(128)}, f32[8,1,128,128]{3,2,1,0:T(8,128)S(1)}, s32[]{:T(128)}, bf16[16,8,1,128,128]{4,3,1,2,0:T(8,128)(2,1)}, s32[]{:T(128)}, /*index=5*/s32[]{:T(128)}, s32[]{:T(128)}, s32[]{:T(128)}) while((s32[]{:T(128)}, f32[8,1,128,128]{3,2,1,0:T(8,128)S(1)}, s32[]{:T(128)}, bf16[16,8,1,128,128]{4,3,1,2,0:T(8,128)(2,1)}, s32[]{:T(128)}, ...), condition=%wide.region_8.9_spmd, body=%wide.region_7.8_spmd.sunk | while | flops 262150 | bytes 1310863 | solution.py:22
  256.0 1.1 convert_add_fusion.5
  257.1 1.1 convert_add_fusion.5
  258.2 1.1 convert_add_fusion.5
  259.3 1.1 convert_add_fusion.5
  260.3 1.1 convert_add_fusion.5
  261.4 1.1 convert_add_fusion.5
  262.5 1.1 convert_add_fusion.5
  263.6 1.1 convert_add_fusion.5
  264.7 1.1 convert_add_fusion.5
  265.8 1.1 convert_add_fusion.5
  266.9 1.1 convert_add_fusion.5
  268.0 1.1 convert_add_fusion.5
  269.1 1.1 convert_add_fusion.5
  270.2 1.1 convert_add_fusion.5
  271.3 1.1 convert_add_fusion.5
  272.4 2.0 fusion.11
  274.3 5.1 %all-to-all-start.1 = ((bf16[8,1,128,128]{3,2,1,0:T(8,128)(2,1)}), bf16[8,1,128,128]{3,2,1,0:T(8,128)(2,1)S(1)}, u32[]{:S(2)}, u32[]{:S(2)}) async-start(bf16[8,1,128,128]{3,2,1,0:T(8,128)(2,1)} %fusion.11), calls=%async_computation.1 | async-start | bytes 524288 | tf_op jit(solution)/shard_map/all_to_all | solution.py:53
  279.4 1.8 fusion.13
  281.2 4.7 %all-to-all-done.1 = bf16[8,1,128,128]{3,2,1,0:T(8,128)(2,1)S(1)} async-done(((bf16[8,1,128,128]{3,2,1,0:T(8,128)(2,1)}), bf16[8,1,128,128]{3,2,1,0:T(8,128)(2,1)S(1)}, u32[]{:S(2)}, u32[]{:S(2)}) %all-to-all-start.1) | async-done | bytes 262176 | tf_op jit(solution)/shard_map/all_to_all | solution.py:53
  285.9 4.4 %all-to-all-start.3 = ((bf16[8,1,128,128]{3,2,1,0:T(8,128)(2,1)}), bf16[8,1,128,128]{3,2,1,0:T(8,128)(2,1)S(1)}, u32[]{:S(2)}, u32[]{:S(2)}) async-start(bf16[8,1,128,128]{3,2,1,0:T(8,128)(2,1)} %fusion.13), calls=%async_computation.3 | async-start | bytes 524288 | tf_op jit(solution)/shard_map/all_to_all | solution.py:54
  290.2 2.5 multiply_convert_fusion.2
  293.4 4.3 %fusion.52 = f32[512,2048]{1,0:T(8,128)} fusion(bf16[512,1024]{0,1:T(8,128)(2,1)S(1)} %bitcast.142, bf16[2048,1024]{1,0:T(8,128)(2,1)S(1)} %copy-done.10), kind=kOutput, calls=%fused_computation.73 | convolution fusion | flops 2147483648 | bytes 9437184 | tf_op jit(solution)/shard_map/dot_general | solution.py:98
  297.7 2.2 multiply_convert_fusion.1
  300.5 2.4 fusion.53
  303.7 1.6 copy-done.13
  305.3 3.7 %add_convert_fusion = bf16[512,2048]{1,0:T(8,128)(2,1)} fusion(f32[512,2048]{1,0:T(8,128)S(1)} %copy-done.15, f32[512,2048]{1,0:T(8,128)S(1)} %fusion.53, bf16[512,1024]{0,1:T(8,128)(2,1)S(1)} %bitcast.141, bf16[2048,1024]{1,0:T(8,128)(2,1)S(1)} %copy-done.13), kind=kOutput, calls=%fused_computation.5 | convolution fusion | flops 2150629376 | bytes 15728640 | tf_op jit(solution)/shard_map/dot_general | solution.py:100
  (51 shorter events, 10.4 us)
Async XLA Ops:
  6.5 1.6 copy-start
  6.5 6.4 %copy-start.12 = (bf16[2048,1024]{1,0:T(8,128)(2,1)S(1)}, bf16[2048,1024]{1,0:T(8,128)(2,1)}, u32[]{:S(2)}) copy-start(bf16[2048,1024]{1,0:T(8,128)(2,1)} %param.14) | copy-start | bytes 12582916
  12.9 2.4 copy-start.2
  15.3 1.0 copy-start.7
  17.7 23.5 %all-to-all-start = ((f32[1,8,128,128]{3,2,0,1:T(8,128)}), f32[1,8,128,128]{3,2,0,1:T(8,128)}, u32[]{:S(2)}, u32[]{:S(2)}) async-start(f32[1,8,128,128]{3,2,0,1:T(8,128)} %convolution_bitcast_fusion.1), calls=%async_computation | async-start | bytes 1048576 | tf_op jit(solution)/shard_map/all_to_all | solution.py:35
  23.5 5.6 %copy-start.9 = (bf16[1024,2048]{1,0:T(8,128)(2,1)S(1)}, bf16[1024,2048]{1,0:T(8,128)(2,1)}, u32[]{:S(2)}) copy-start(bf16[1024,2048]{1,0:T(8,128)(2,1)} %param.15) | copy-start | bytes 12582916
  23.5 5.6 %copy-start.14 = (bf16[512,2048]{1,0:T(8,128)(2,1)S(1)}, bf16[512,2048]{1,0:T(8,128)(2,1)}, u32[]{:S(2)}) copy-start(bf16[512,2048]{1,0:T(8,128)(2,1)} %param.11) | copy-start | bytes 6291460
  33.9 33.3 %copy-start.1 = (bf16[512,1024]{0,1:T(8,128)(2,1)}, bf16[512,1024]{0,1:T(8,128)(2,1)S(1)}, u32[]{:S(2)}) copy-start(bf16[512,1024]{0,1:T(8,128)(2,1)S(1)} %copy.47) | copy-start | bytes 3145732
  41.1 14.3 %all-to-all-start.2 = ((f32[8,1,1,128,128]{4,3,2,1,0:T(8,128)}), f32[8,1,1,128,128]{4,3,2,1,0:T(8,128)}, u32[]{:S(2)}, u32[]{:S(2)}) async-start(f32[8,1,1,128,128]{4,3,2,1,0:T(8,128)} %fusion.43), calls=%async_computation.2 | async-start | bytes 1048576 | tf_op jit(solution)/shard_map/all_to_all | solution.py:37
  57.2 91.1 %all-reduce.3.cloned.1.call-start = ((), (), s32[]{:S(2)}) async-start(), calls=%async_computation.6 | async-start | bytes 2097152 | tf_op jit(solution)/shard_map/psum | solution.py:43
  57.9 144.7 %all-gather.5.cloned.1.call-start = ((), (), s32[]{:S(2)}) async-start(), calls=%async_computation.4 | async-start | bytes 4456448 | tf_op jit(solution)/shard_map/all_gather | solution.py:15
  58.7 197.3 %all-gather.7.cloned.1.call-start = ((), (), s32[]{:S(2)}) async-start(), calls=%async_computation.5 | async-start | bytes 4456448 | tf_op jit(solution)/shard_map/all_gather | solution.py:15
  59.4 2.8 copy-start.5
  62.2 2.2 copy-start.3
  274.3 11.6 %all-to-all-start.1 = ((bf16[8,1,128,128]{3,2,1,0:T(8,128)(2,1)}), bf16[8,1,128,128]{3,2,1,0:T(8,128)(2,1)S(1)}, u32[]{:S(2)}, u32[]{:S(2)}) async-start(bf16[8,1,128,128]{3,2,1,0:T(8,128)(2,1)} %fusion.11), calls=%async_computation.1 | async-start | bytes 524288 | tf_op jit(solution)/shard_map/all_to_all | solution.py:53
  285.9 11.8 %all-to-all-start.3 = ((bf16[8,1,128,128]{3,2,1,0:T(8,128)(2,1)}), bf16[8,1,128,128]{3,2,1,0:T(8,128)(2,1)S(1)}, u32[]{:S(2)}, u32[]{:S(2)}) async-start(bf16[8,1,128,128]{3,2,1,0:T(8,128)(2,1)} %fusion.13), calls=%async_computation.3 | async-start | bytes 524288 | tf_op jit(solution)/shard_map/all_to_all | solution.py:54
  290.2 3.1 copy-start.10
  293.4 4.3 %copy-start.8 = (bf16[64,8,8,128]{3,2,1,0:T(8,128)(2,1)S(1)}, bf16[64,8,8,128]{3,2,1,0:T(8,128)(2,1)}, u32[]{:S(2)}) copy-start(bf16[64,8,8,128]{3,2,1,0:T(8,128)(2,1)} %copy-done.7) | copy-start | bytes 3145732
  297.7 2.8 copy-start.11
  300.5 2.4 copy-start.4
  300.5 2.4 copy-start.6
  300.5 3.2 copy-start.15
  302.9 2.4 copy-start.13
Sparse Core Ops, SparseCore 0:
  61.3 86.9 all-reduce.2
  150.5 52.1 all-gather.4
  204.8 51.0 all-gather.6
